TPU v7x, 128 devices: a whole 4x4x4 slice. The times are simulated.
128 devices in a mesh: seq: 16 (over x_lo, y, core), heads: 8 (over z, x_hi).
Axes of the slice: x: 4 (x_hi: 2, x_lo: 2; x = x_hi * 2 + x_lo), y: 4, z: 4, core: 2. Of those that a mesh axis runs over, the one named last changes fastest.
Arguments:
- hidden_in: bfloat16 [4096, 8192], P('seq', 'heads'), may hold values from -6 to 6
- queries: bfloat16 [4096, 8192], P('seq', 'heads'), as said below
- image_kv: bfloat16 [16, 2, 6528, 1024], P('seq', None, None, 'heads'), as said below
- out_weight: bfloat16 [8192, 8192], P('seq', 'heads'), may hold values from -0.0625 to 0.0625
- gate: float32 [1], replicated, may hold values from 0.4 to 1.2
- tile_counts: int32 [16], replicated, may hold values from 1 to 4, as said below
- owners: int32 [256], replicated, may hold values from 0 to 15, as said below
- starts: int32 [256], replicated, may hold values from 0 to 3, as said below
- norm_gain: float32 [8192], P('heads'), may hold values from 0.1 to 1.9
- norm_grad: bfloat16 [4096, 8192], P('seq', 'heads'), may hold values from -6 to 6
- stream_grad: bfloat16 [4096, 8192], P('seq', 'heads'), may hold values from -6 to 6
Outputs:
- hidden_out: bfloat16 [4096, 8192], P('seq', 'heads')
- stream_in_grad: float32 [4096, 8192], P('seq', 'heads')
Inputs may be any that keep to these rules, and one draw needn't show every extreme that they name: `tile_counts`: tiles of each image; some image has 4 tiles in every draw. `owners`: the image (named by the seq index that owns it) that a block of 16 text rows attends to; of the 16 blocks of one seq index at most 2 name the same image, and in every draw some image is named by exactly 2 blocks of every seq index. `starts`: the first tile a block sees, below the tile count of the block's image; in every draw some block starts at tile 0 and some at tile 4 - 1. `image_kv`: keys and values are real-valued. real-valued queries.
All inputs are finite; a program needn't handle non-finite values.
Results may differ from a plain program's by a relative error of at most 0.007.
Values may be sent and summed in bfloat16 or wider, within the bound.
No kernel may reach another device: no remote copies, remote signals or barrier semaphores. Data moves between devices by JAX's collectives and lax.ppermute only.
A program may use at most 128 MiB of HBM per device.

v0:
```python
import math

import jax
import jax.numpy as jnp
from jax import lax
from jax.experimental import pallas as pl
from jax.experimental.pallas import tpu as pltpu
from jax.sharding import Mesh, PartitionSpec as P


D = 8192
HEAD_DIM = 128
TILE_TOK = 1601
TILE_STEP = 1600
KEY_CAP = 6528
KEY_BLK = 1664
BLOCKS_DEV = 16
CAP = 2
BLK = 16
SEQ = 16
SLOTS = SEQ * CAP
HEADS_DEV = 8
GROUP = 8
SUB = 512
LOW = -2.3e38
HIGH = 2.3e38
EPS = 1e-05
EXP2_SCALE = math.log2(math.e) / math.sqrt(HEAD_DIM)

SEQ_AXES = ("xl", "y", "core")
HEAD_AXES = ("z", "xh")
UP = [(i, (i + 1) % 4) for i in range(4)]
DOWN = [(i, (i - 1) % 4) for i in range(4)]
SWAP = [(0, 1), (1, 0)]
SLANT = [(a * 4 + b, (1 - a) * 4 + (b + 1) % 4) for a in range(2) for b in range(4)]


def vmem():
    return pl.BlockSpec(memory_space=pltpu.VMEM)


def smem():
    return pl.BlockSpec(memory_space=pltpu.SMEM)


def near(*arrays):
    return [pltpu.with_memory_space_constraint(x, pltpu.VMEM) for x in arrays]


LIMIT = pltpu.CompilerParams(vmem_limit_bytes=28 << 20)
SMALL = pltpu.CompilerParams(vmem_limit_bytes=12 << 20)


def dispatch_kernel(owner_ref, q_ref, out_ref, used, sems):
    first = lax.axis_index(SEQ_AXES) * BLOCKS_DEV
    for o in range(SEQ):
        used[o] = 0

    copies = []
    for b in range(BLOCKS_DEV):
        o = owner_ref[first + b]
        r = used[o]
        used[o] = r + 1
        block = q_ref.at[b * BLK : (b + 1) * BLK, :]
        copies.append(pltpu.make_async_copy(block, out_ref.at[o, r], sems.at[b]))
        copies[-1].start()
    for copy in copies:
        copy.wait()


def dispatch(owners, queries):
    return pl.pallas_call(
        dispatch_kernel,
        out_shape=pltpu.VMEM((SEQ, CAP, BLK, queries.shape[1]), queries.dtype),
        in_specs=[smem(), pl.BlockSpec(memory_space=pltpu.HBM)],
        out_specs=vmem(),
        scratch_shapes=[pltpu.SMEM((SEQ,), jnp.int32), pltpu.SemaphoreType.DMA((BLOCKS_DEV,))],
        compiler_params=SMALL,
        name="dispatch",
    )(owners, pltpu.with_memory_space_constraint(queries, pltpu.HBM))


def collect_kernel(owner_ref, c_ref, out_ref, used):
    core = lax.axis_index("core")
    first = (lax.axis_index(SEQ_AXES) - core) * BLOCKS_DEV
    for part in range(2):
        which = jnp.bitwise_xor(core, part)
        for o in range(SEQ):
            used[o] = 0

        def place(b, carry):
            o = owner_ref[first + which * BLOCKS_DEV + b]
            r = used[o]
            used[o] = r + 1
            row = pl.multiple_of((part * BLOCKS_DEV + b) * BLK, BLK)
            out_ref[pl.ds(row, BLK), :] = c_ref[o, which * CAP + r]
            return carry

        lax.fori_loop(0, BLOCKS_DEV, place, 0)


def collect(owners, returned):
    rows = 2 * BLOCKS_DEV * BLK
    return pl.pallas_call(
        collect_kernel,
        out_shape=pltpu.VMEM((rows, returned.shape[-1]), returned.dtype),
        in_specs=[smem(), vmem()],
        out_specs=vmem(),
        scratch_shapes=[pltpu.SMEM((SEQ,), jnp.int32)],
        compiler_params=SMALL,
        name="collect",
    )(owners, *near(returned))


def attend_kernel(order, first, meta, q_ref, kv_ref, o_ref, k_s, v_s, q_s, m_s, acc, sems):
    load_k = pltpu.make_async_copy(kv_ref.at[0, 0], k_s, sems.at[0])
    load_v = pltpu.make_async_copy(kv_ref.at[0, 1], v_s.at[:, :HEAD_DIM], sems.at[1])
    load_k.start()
    load_v.start()
    v_s[:, HEAD_DIM:] = jnp.ones((KEY_CAP, HEAD_DIM), jnp.bfloat16)
    load_k.wait()
    load_v.wait()
    groups = lax.div(meta[0] + GROUP - 1, GROUP)
    tiles = meta[1]
    rows = GROUP * HEADS_DEV * BLK
    slot_rows = HEADS_DEV * BLK
    col = lax.broadcasted_iota(jnp.int32, (SUB, HEAD_DIM), 1)

    def group(g, carry):
        for i in range(GROUP):
            slot = order[g * GROUP + i]
            for h in range(HEADS_DEV):
                at = i * slot_rows + h * BLK
                q_s[at : at + BLK, :] = q_ref[slot, :, h * HEAD_DIM : (h + 1) * HEAD_DIM]
        m_s[...] = jnp.full_like(m_s, LOW)
        acc[...] = jnp.zeros_like(acc)

        def tile(t, inner):
            base = pl.multiple_of(t * TILE_STEP, BLK)
            keys = k_s[pl.ds(base, KEY_BLK), :]
            blocks = rows // SUB

            def scores(u):
                return lax.dot_general(
                    q_s[u * SUB : (u + 1) * SUB, :],
                    keys,
                    (((1,), (1,)), ((), ())),
                    preferred_element_type=jnp.float32,
                )

            ahead = scores(0)
            for u in range(blocks):
                part = slice(u * SUB, (u + 1) * SUB)
                s = ahead
                if u + 1 < blocks:
                    ahead = scores(u + 1)
                tail = KEY_BLK - HEAD_DIM
                head_cols = jnp.where(col >= t, s[:, :HEAD_DIM], LOW)
                tail_cols = jnp.where(col + tail < t + TILE_TOK, s[:, tail:], LOW)
                s = jnp.concatenate([head_cols, s[:, HEAD_DIM:tail], tail_cols], axis=1)
                old = m_s[part, :1]
                new = jnp.maximum(old, jnp.max(s, axis=1, keepdims=True))
                kept, shifts = [], []
                for i in range(SUB // slot_rows):
                    seen = first[g * GROUP + u * (SUB // slot_rows) + i] <= t
                    cut = slice(i * slot_rows, (i + 1) * slot_rows)
                    kept.append(jnp.where(seen, new[cut], old[cut]))
                    shifts.append(jnp.where(seen, new[cut], HIGH))
                new = jnp.concatenate(kept, axis=0)
                high = jnp.concatenate(shifts, axis=0)
                probs = jnp.exp2((s - high) * EXP2_SCALE).astype(jnp.bfloat16)
                fade = jnp.exp2((old - new) * EXP2_SCALE)
                m_s[part, :] = jnp.broadcast_to(new, (SUB, HEAD_DIM))
                acc[part, :] = acc[part, :] * fade + jnp.dot(
                    probs,
                    v_s[pl.ds(base, KEY_BLK), :],
                    preferred_element_type=jnp.float32,
                )
            return inner

        lax.fori_loop(first[g * GROUP], tiles, tile, 0)
        for i in range(GROUP):
            slot = order[g * GROUP + i]
            chip = lax.shift_right_logical(slot, 2)
            place = jnp.bitwise_and(slot, 3)
            for h in range(HEADS_DEV):
                at = i * slot_rows + h * BLK
                cut = slice(at, at + BLK)
                half, inside = divmod(h, HEADS_DEV // 2)
                o_ref[chip, half, place, :, inside * HEAD_DIM : (inside + 1) * HEAD_DIM] = (
                    acc[cut, :HEAD_DIM] / acc[cut, HEAD_DIM:]
                ).astype(jnp.bfloat16)
        return carry

    lax.fori_loop(0, groups, group, 0)


def attend(order, first, meta, received, image_kv):
    rows = GROUP * HEADS_DEV * BLK
    return pl.pallas_call(
        attend_kernel,
        out_shape=pltpu.VMEM((SEQ // 2, 2, 2 * CAP, BLK, HEADS_DEV * HEAD_DIM // 2), jnp.bfloat16),
        in_specs=[smem()] * 3 + [vmem(), pl.BlockSpec(memory_space=pltpu.HBM)],
        out_specs=vmem(),
        scratch_shapes=[
            pltpu.VMEM((KEY_CAP, HEAD_DIM), jnp.bfloat16),
            pltpu.VMEM((KEY_CAP, 2 * HEAD_DIM), jnp.bfloat16),
            pltpu.VMEM((rows, HEAD_DIM), jnp.bfloat16),
            pltpu.VMEM((rows, HEAD_DIM), jnp.float32),
            pltpu.VMEM((rows, 2 * HEAD_DIM), jnp.float32),
            pltpu.SemaphoreType.DMA((2,)),
        ],
        compiler_params=LIMIT,
        cost_estimate=pl.CostEstimate(flops=10**10, transcendentals=10**7, bytes_accessed=10**7),
        name="attend",
    )(
        order,
        first,
        meta,
        *near(received),
        pltpu.with_memory_space_constraint(image_kv, pltpu.HBM),
    )


def assemble_kernel(*refs):
    pieces, out_ref = refs[:-1], refs[-1]
    xl = lax.axis_index("xl")
    y = lax.axis_index("y")
    n = 0
    for col in range(2):
        for dy in (0, 3, 1, 2):
            at = jnp.bitwise_xor(xl, col) * 4 + jnp.bitwise_and(y + dy, 3)
            row = 0
            while row < 512:
                size = pieces[n].shape[0]
                out_ref[at, row : row + size, :] = pieces[n][...]
                row += size
                n += 1


def assemble(pieces):
    return pl.pallas_call(
        assemble_kernel,
        out_shape=pltpu.VMEM((8,) + (512, pieces[0].shape[1]), pieces[0].dtype),
        in_specs=[vmem()] * len(pieces),
        out_specs=vmem(),
        compiler_params=SMALL,
        name="assemble",
    )(*near(*pieces))


def weight_spot(dz, flip):
    z = jnp.bitwise_and(lax.axis_index("z") + dz, 3)
    return z * 2 + jnp.bitwise_xor(lax.axis_index("xh"), flip)


def project_first_kernel(own, below, above, across, w, out_ref):
    total = None
    for block, dz, flip in ((own, 0, 0), (below, 3, 0), (above, 1, 0), (across, 0, 1)):
        term = jnp.dot(block[...], w[weight_spot(dz, flip)], preferred_element_type=jnp.float32)
        total = term if total is None else total + term
    out_ref[...] = total


def project_first(own, below, above, across, weights):
    return pl.pallas_call(
        project_first_kernel,
        out_shape=pltpu.VMEM((own.shape[0], weights.shape[2]), jnp.float32),
        in_specs=[vmem()] * 5,
        out_specs=vmem(),
        compiler_params=LIMIT,
        name="project_first",
    )(*near(own, below, above, across, weights))


def project_last_kernel(below, above, far_a, far_b, over_a, over_b, w, total, keep_ref, give_ref):
    half = keep_ref.shape[0]
    full = total[...]
    far = jnp.concatenate([far_a[...], far_b[...]], axis=0)
    over = jnp.concatenate([over_a[...], over_b[...]], axis=0)
    for block, dz, flip in ((below[...], 3, 1), (above[...], 1, 1), (far, 2, 0), (over, 2, 1)):
        full += jnp.dot(block, w[weight_spot(dz, flip)], preferred_element_type=jnp.float32)
    keep_ref[...] = full[:half]
    give_ref[...] = full[half:].astype(jnp.bfloat16)


def project_last(blocks, weights, total):
    shape = pltpu.VMEM((total.shape[0] // 2, total.shape[1]), jnp.float32)
    return pl.pallas_call(
        project_last_kernel,
        out_shape=(shape, pltpu.VMEM(shape.shape, jnp.bfloat16)),
        in_specs=[vmem()] * 8,
        out_specs=(vmem(), vmem()),
        compiler_params=LIMIT,
        name="project_last",
    )(*near(*blocks, weights, total))


def routing(owners, starts, here):
    owner_table = owners.reshape(SEQ, BLOCKS_DEV)
    start_table = starts.reshape(SEQ, BLOCKS_DEV)
    ids = jnp.arange(BLOCKS_DEV)
    arriving = owner_table == here
    earlier = ids[None, :] < ids[:, None]
    rank = jnp.sum((arriving[:, None, :] & earlier[None, :, :]).astype(jnp.int32), axis=2)
    hit = arriving[:, None, :] & (rank[:, None, :] == jnp.arange(CAP)[None, :, None])
    slot_start = jnp.sum(jnp.where(hit, start_table[:, None, :], 0), axis=2).reshape(SLOTS)
    active = jnp.any(hit, axis=2).reshape(SLOTS)
    slots = jnp.arange(SLOTS)
    key = jnp.where(active, slot_start, 8) * SLOTS + slots
    position = jnp.sum((key[None, :] < key[:, None]).astype(jnp.int32), axis=1)
    at = position[None, :] == slots[:, None]
    order = jnp.sum(jnp.where(at, slots[None, :], 0), axis=1)
    first = jnp.sum(jnp.where(at, slot_start[None, :], 0), axis=1)
    return order, first, jnp.sum(active.astype(jnp.int32))


def local(
    hidden_in,
    queries,
    image_kv,
    out_weight,
    gate,
    tile_counts,
    owners,
    starts,
    norm_gain,
    norm_grad,
    stream_grad,
):
    here = lax.axis_index(SEQ_AXES)
    width = queries.shape[1]
    half = out_weight.shape[0] // 2

    w = out_weight
    outgoing = dispatch(owners, queries)
    received = lax.all_to_all(outgoing, SEQ_AXES, split_axis=0, concat_axis=0, tiled=True)

    w_lo = lax.ppermute(w, "y", UP)
    w_hi = lax.ppermute(w, "y", DOWN)
    w_x = lax.ppermute(w, "xl", SWAP)
    x_lo = lax.ppermute(w, ("xl", "y"), SLANT)

    order, first, n_active = routing(owners, starts, here)
    tiles = lax.dynamic_index_in_dim(tile_counts, here, 0, keepdims=False)
    meta = jnp.stack([n_active, tiles])
    slots = received.reshape(SLOTS, BLK, width)
    context = attend(order, first, meta, slots, image_kv)
    w_far = lax.ppermute(w_lo, "y", UP)
    x_hi = lax.ppermute(w_x, "y", DOWN)


    x_lo_top, x_hi_end = x_lo[:half], x_hi[half:]
    x_far_a = lax.ppermute(x_lo_top, "y", UP)
    x_far_b = lax.ppermute(x_hi_end, "y", DOWN)

    context = context.reshape(SEQ, 2 * CAP, BLK, width // 2)
    returned = lax.all_to_all(context, SEQ_AXES, split_axis=0, concat_axis=0, tiled=True)
    weights = assemble((w, w_lo, w_hi, w_far, w_x, x_lo, x_hi, x_far_a, x_far_b))
    own = collect(owners, returned)
    below = lax.ppermute(own, "z", UP)
    above = lax.ppermute(own, "z", DOWN)
    across = lax.ppermute(own, "xh", SWAP)
    rows = own.shape[0] // 2
    far_a = lax.ppermute(below[:rows], "z", UP)
    far_b = lax.ppermute(above[rows:], "z", DOWN)
    across_below = lax.ppermute(across, "z", UP)
    across_above = lax.ppermute(across, "z", DOWN)
    over_a = lax.ppermute(far_a, "xh", SWAP)
    over_b = lax.ppermute(far_b, "xh", SWAP)
    total = project_first(own, below, above, across, weights)
    blocks = (across_below, across_above, far_a, far_b, over_a, over_b)
    keep, give = project_last(blocks, weights, total)
    branch = keep + lax.ppermute(give, "core", SWAP).astype(jnp.float32)

    hidden_out = (hidden_in.astype(jnp.float32) + jnp.tanh(gate[0]) * branch).astype(jnp.bfloat16)
    hidden = hidden_out.astype(jnp.float32)
    scaled = norm_gain[None, :] * norm_grad.astype(jnp.float32)
    sums = jnp.stack([jnp.sum(hidden * hidden, axis=1), jnp.sum(hidden * scaled, axis=1)])
    copies = jnp.broadcast_to(sums[None], (8,) + sums.shape)
    copies = lax.all_to_all(copies, HEAD_AXES, split_axis=0, concat_axis=0, tiled=True)
    squares, product = jnp.sum(copies, axis=0)
    inverse = lax.rsqrt(squares / D + EPS)[:, None]
    project_mean = (product / D)[:, None]
    stream_in_grad = (
        stream_grad.astype(jnp.float32) + inverse * scaled - inverse**3 * project_mean * hidden
    )
    return (hidden_out, stream_in_grad)


def solution(mesh):
    fine = Mesh(mesh.devices.reshape(2, 4, 2, 4, 2), SEQ_AXES + HEAD_AXES)
    both = P(SEQ_AXES, HEAD_AXES)
    placed = (
        both,
        both,
        P(SEQ_AXES, None, None, HEAD_AXES),
        both,
        P(),
        P(),
        P(),
        P(),
        P(HEAD_AXES),
        both,
        both,
    )
    return jax.shard_map(
        local,
        mesh=fine,
        in_specs=placed,
        out_specs=(both, both),
        check_vma=False,
    )
```

profile of v0, /device:TPU:0, one launch (start us, length us, event | category | flops | bytes accessed | tf_op | source)
XLA Modules:
  0.0 188.4 jit_solution(6890037694097546224)
XLA Ops:
  0.6 1.7 collective-permute-start.12
  2.3 1.6 collective-permute-start.9
  3.9 0.7 copy-done
  4.6 2.7 %dispatch.1 = bf16[16,2,16,1024]{3,2,1,0:T(8,128)(2,1)} custom-call(s32[256]{0:T(256)S(1)} %copy-done, bf16[256,1024]{1,0:T(8,128)(2,1)} %q_ref.1), custom_call_target="tpu_custom_call" | custom-call | tf_op jit(solution)/shard_map/dispatch/pallas_call | solution.py:72
  7.3 4.3 %all-to-all-start = ((bf16[16,2,16,1024]{3,2,1,0:T(8,128)(2,1)}), bf16[16,2,16,1024]{3,2,1,0:T(8,128)(2,1)S(1)}, u32[]{:S(2)}, u32[]{:S(2)}) async-start(bf16[16,2,16,1024]{3,2,1,0:T(8,128)(2,1)} %dispatch.1), calls=%async_computation | async-start | bytes 2097152 | tf_op jit(solution)/shard_map/all_to_all | solution.py:337
  11.6 0.1 eq.41
  11.8 0.4 convert_reduce_fusion
  12.2 0.1 select_reduce_fusion.2
  12.3 0.1 copy.16
  12.4 0.1 reshape.100
  12.5 0.1 fusion.4
  12.6 0.1 copy.15
  12.7 0.1 reshape.99
  12.8 0.6 dynamic_slice.4
  13.4 0.6 convert_reduce_fusion.2
  14.0 1.3 pad_add_fusion.meta
  15.3 0.2 convert_reduce_fusion.1
  15.5 0.1 select_reduce_fusion
  15.6 24.3 %all-to-all-done = bf16[16,2,16,1024]{3,2,1,0:T(8,128)(2,1)S(1)} async-done(((bf16[16,2,16,1024]{3,2,1,0:T(8,128)(2,1)}), bf16[16,2,16,1024]{3,2,1,0:T(8,128)(2,1)S(1)}, u32[]{:S(2)}, u32[]{:S(2)}) %all-to-all-start) | async-done | bytes 1048608 | tf_op jit(solution)/shard_map/all_to_all | solution.py:337
  39.9 30.0 %attend.1 = bf16[8,2,4,16,512]{4,3,2,1,0:T(8,128)(2,1)} custom-call(s32[32]{0:T(128)S(1)} %get-tuple-element.9.order, s32[32]{0:T(128)S(1)} %get-tuple-element.8.first, s32[2]{0:T(128)S(1)} %pad_add_fusion.meta, bf16[32,16,1024]{2,1,0:T(8,128)(2,1)S(1)} %bitcast.8, bf16[1,2,6528,128]{3,2,1,0:T(8,128)(2,1)} %kv_ref.1), custom_call_target="tpu_custom_call" | custom-call | flops 10000000000 | bytes 10000000 | tf_op jit(solution)/shard_map/attend/pallas_call | solution.py:200
  69.9 3.7 %all-to-all-start.1 = ((bf16[16,4,16,512]{3,2,1,0:T(8,128)(2,1)}), bf16[16,4,16,512]{3,2,1,0:T(8,128)(2,1)S(1)}, u32[]{:S(2)}, u32[]{:S(2)}) async-start(bf16[16,4,16,512]{3,2,1,0:T(8,128)(2,1)} %bitcast.3), calls=%async_computation.1 | async-start | bytes 2097152 | tf_op jit(solution)/shard_map/all_to_all | solution.py:358
  73.6 2.8 %collective-permute-start.13 = (bf16[512,1024]{1,0:T(8,128)(2,1)}, bf16[512,1024]{1,0:T(8,128)(2,1)S(1)}, u32[]{:S(2)}, u32[]{:S(2)}) collective-permute-start(bf16[512,1024]{1,0:T(8,128)(2,1)} %refs_0_.1), channel_id=1, source_target_pairs={{0,80},{16,96},{32,112},{48,64},{64,16},{80,32},{96,48},{112,0},{1... | collective-permute-start | bytes 3145736 | tf_op jit(solution)/shard_map/ppermute | solution.py:342
  76.3 1.8 collective-permute-start.14
  78.1 1.5 collective-permute-start.10
  79.6 11.0 %all-to-all-done.1.c_ref = bf16[16,4,16,512]{3,2,1,0:T(8,128)(2,1)S(1)} async-done(((bf16[16,4,16,512]{3,2,1,0:T(8,128)(2,1)}), bf16[16,4,16,512]{3,2,1,0:T(8,128)(2,1)S(1)}, u32[]{:S(2)}, u32[]{:S(2)}) %all-to-all-start.1) | async-done | bytes 1048608 | tf_op jit(solution)/shard_map/all_to_all | solution.py:358
  90.6 1.0 collect.1.own
  91.6 2.0 %collective-permute-start.3 = (bf16[512,512]{1,0:T(8,128)(2,1)S(1)}, bf16[512,512]{1,0:T(8,128)(2,1)S(1)}, u32[]{:S(2)}, u32[]{:S(2)}) collective-permute-start(bf16[512,512]{1,0:T(8,128)(2,1)S(1)} %collect.1.own), channel_id=1, source_target_pairs={{0,2},{2,4},{4,6},{6,0},{1,3},{3,5},{5,7},{7,1},{8,10},{10,12},{12... | collective-permute-start | bytes 1572872 | tf_op jit(solution)/shard_map/ppermute | solution.py:361
  93.6 18.9 %collective-permute-done.13.refs_5_ = bf16[512,1024]{1,0:T(8,128)(2,1)S(1)} collective-permute-done((bf16[512,1024]{1,0:T(8,128)(2,1)}, bf16[512,1024]{1,0:T(8,128)(2,1)S(1)}, u32[]{:S(2)}, u32[]{:S(2)}) %collective-permute-start.13) | collective-permute-done | bytes 1048608 | tf_op jit(solution)/shard_map/ppermute | solution.py:342
  112.5 4.0 %collective-permute-start.5 = (bf16[512,512]{1,0:T(8,128)(2,1)S(1)}, bf16[512,512]{1,0:T(8,128)(2,1)S(1)}, u32[]{:S(2)}, u32[]{:S(2)}) collective-permute-start(bf16[512,512]{1,0:T(8,128)(2,1)S(1)} %collect.1.own), channel_id=1, source_target_pairs={{0,6},{2,0},{4,2},{6,4},{1,7},{3,1},{5,3},{7,5},{8,14},{10,8},{12,... | collective-permute-start | bytes 1572872 | tf_op jit(solution)/shard_map/ppermute | solution.py:362
  116.7 3.0 %collective-permute-start = (bf16[512,512]{1,0:T(8,128)(2,1)S(1)}, bf16[512,512]{1,0:T(8,128)(2,1)S(1)}, u32[]{:S(2)}, u32[]{:S(2)}) collective-permute-start(bf16[512,512]{1,0:T(8,128)(2,1)S(1)} %collect.1.own), channel_id=1, source_target_pairs={{0,1},{1,0},{2,3},{3,2},{4,5},{5,4},{6,7},{7,6},{8,9},{9,8},{10,11... | collective-permute-start | bytes 1572872 | tf_op jit(solution)/shard_map/ppermute | solution.py:363
  119.8 7.6 %collective-permute-done.5.above = bf16[512,512]{1,0:T(8,128)(2,1)S(1)} collective-permute-done((bf16[512,512]{1,0:T(8,128)(2,1)S(1)}, bf16[512,512]{1,0:T(8,128)(2,1)S(1)}, u32[]{:S(2)}, u32[]{:S(2)}) %collective-permute-start.5) | collective-permute-done | bytes 524320 | tf_op jit(solution)/shard_map/ppermute | solution.py:362
  127.5 0.9 collective-permute-start.16
  128.4 5.0 %collective-permute-done.10.refs_2_ = bf16[512,1024]{1,0:T(8,128)(2,1)} collective-permute-done((bf16[512,1024]{1,0:T(8,128)(2,1)}, bf16[512,1024]{1,0:T(8,128)(2,1)}, u32[]{:S(2)}, u32[]{:S(2)}) %collective-permute-start.10) | collective-permute-done | bytes 1048608 | tf_op jit(solution)/shard_map/ppermute | solution.py:340
  133.5 1.9 %collective-permute-start.4 = (bf16[256,512]{1,0:T(8,128)(2,1)S(1)}, bf16[256,512]{1,0:T(8,128)(2,1)S(1)}, u32[]{:S(2)}, u32[]{:S(2)}) collective-permute-start(bf16[256,512]{1,0:T(8,128)(2,1)S(1)} %slice.16), channel_id=1, source_target_pairs={{0,2},{2,4},{4,6},{6,0},{1,3},{3,5},{5,7},{7,1},{8,10},{10,12},{12... | collective-permute-start | bytes 786440 | tf_op jit(solution)/shard_map/ppermute | solution.py:365
  135.4 10.9 %collective-permute-done.15.refs_7_ = bf16[256,1024]{1,0:T(8,128)(2,1)S(1)} collective-permute-done((bf16[256,1024]{1,0:T(8,128)(2,1)S(1)}, bf16[256,1024]{1,0:T(8,128)(2,1)S(1)}, u32[]{:S(2)}, u32[]{:S(2)}) %collective-permute-start.15) | collective-permute-done | bytes 524320 | tf_op jit(solution)/shard_map/ppermute | solution.py:354
  146.2 4.0 %collective-permute-start.6 = (bf16[256,512]{1,0:T(8,128)(2,1)S(1)}, bf16[256,512]{1,0:T(8,128)(2,1)S(1)}, u32[]{:S(2)}, u32[]{:S(2)}) collective-permute-start(bf16[256,512]{1,0:T(8,128)(2,1)S(1)} %slice.17), channel_id=1, source_target_pairs={{0,6},{2,0},{4,2},{6,4},{1,7},{3,1},{5,3},{7,5},{8,14},{10,8},{12,... | collective-permute-start | bytes 786440 | tf_op jit(solution)/shard_map/ppermute | solution.py:366
  150.3 3.2 %collective-permute-start.2 = (bf16[512,512]{1,0:T(8,128)(2,1)S(1)}, bf16[512,512]{1,0:T(8,128)(2,1)S(1)}, u32[]{:S(2)}, u32[]{:S(2)}) collective-permute-start(bf16[512,512]{1,0:T(8,128)(2,1)S(1)} %collective-permute-done.across), channel_id=1, source_target_pairs={{0,6},{2,0},{4,2},{6,4},{1,7},{3,1},{5,3},{7,5},{8,14},{10,8},{12,... | collective-permute-start | bytes 1572872 | tf_op jit(solution)/shard_map/ppermute | solution.py:368
  153.5 3.0 %collective-permute-start.7 = (bf16[256,512]{1,0:T(8,128)(2,1)S(1)}, bf16[256,512]{1,0:T(8,128)(2,1)S(1)}, u32[]{:S(2)}, u32[]{:S(2)}) collective-permute-start(bf16[256,512]{1,0:T(8,128)(2,1)S(1)} %collective-permute-done.4.far_a), channel_id=1, source_target_pairs={{0,1},{1,0},{2,3},{3,2},{4,5},{5,4},{6,7},{7,6},{8,9},{9,8},{10,11... | collective-permute-start | bytes 786440 | tf_op jit(solution)/shard_map/ppermute | solution.py:369
  156.5 0.5 collective-permute-done.6.far_b
  157.0 3.0 %collective-permute-start.8 = (bf16[256,512]{1,0:T(8,128)(2,1)S(1)}, bf16[256,512]{1,0:T(8,128)(2,1)S(1)}, u32[]{:S(2)}, u32[]{:S(2)}) collective-permute-start(bf16[256,512]{1,0:T(8,128)(2,1)S(1)} %collective-permute-done.6.far_b), channel_id=1, source_target_pairs={{0,1},{1,0},{2,3},{3,2},{4,5},{5,4},{6,7},{7,6},{8,9},{9,8},{10,11... | collective-permute-start | bytes 786440 | tf_op jit(solution)/shard_map/ppermute | solution.py:370
  159.9 2.7 %assemble.1.w = bf16[8,512,1024]{2,1,0:T(8,128)(2,1)S(1)} custom-call(bf16[512,1024]{1,0:T(8,128)(2,1)} %refs_0_.1, bf16[512,1024]{1,0:T(8,128)(2,1)} %collective-permute-done.9.refs_1_, bf16[512,1024]{1,0:T(8,128)(2,1)} %collective-permute-done.10.refs_2_, bf16[512,1024]{1,0:T(8,128)(2,1)S(1)} %collective-permute-done.11.refs_3_, ...), custom_call_target="tpu_custom_call" | custom-call | tf_op jit(solution)/shard_map/assemble/pallas_call | solution.py:242
  162.7 2.3 %project_first.1.total = f32[512,1024]{1,0:T(8,128)S(1)} custom-call(bf16[512,512]{1,0:T(8,128)(2,1)S(1)} %collect.1.own, bf16[512,512]{1,0:T(8,128)(2,1)S(1)} %collective-permute-done.3.below, bf16[512,512]{1,0:T(8,128)(2,1)S(1)} %collective-permute-done.5.above, bf16[512,512]{1,0:T(8,128)(2,1)S(1)} %collective-permute-done.across, ...), custom_call_target="tpu_custom_call" | custom-call | tf_op jit(solution)/shard_map/project_first/pallas_call | solution.py:266
  165.1 3.1 %collective-permute-done.8.over_b = bf16[256,512]{1,0:T(8,128)(2,1)S(1)} collective-permute-done((bf16[256,512]{1,0:T(8,128)(2,1)S(1)}, bf16[256,512]{1,0:T(8,128)(2,1)S(1)}, u32[]{:S(2)}, u32[]{:S(2)}) %collective-permute-start.8) | collective-permute-done | bytes 262176 | tf_op jit(solution)/shard_map/ppermute | solution.py:370
  168.1 2.3 %project_last.1 = (f32[256,1024]{1,0:T(8,128)S(1)}, bf16[256,1024]{1,0:T(8,128)(2,1)S(1)}) custom-call(bf16[512,512]{1,0:T(8,128)(2,1)S(1)} %collective-permute-done.1.below, bf16[512,512]{1,0:T(8,128)(2,1)S(1)} %collective-permute-done.2.above, bf16[256,512]{1,0:T(8,128)(2,1)S(1)} %collective-permute-done.4.far_a, ...), custom_call_target="tpu_custom_call" | custom-call | tf_op jit(solution)/shard_map/project_last/pallas_call | solution.py:289
  171.3 1.2 collective-permute-done.17
  172.5 0.5 fusion
  173.0 14.1 %all_to_all.15 = f32[8,2,256]{2,1,0:T(2,128)S(1)} all-to-all(f32[8,2,256]{2,1,0:T(2,128)S(1)} %broadcast_in_dim.64), channel_id=1, replica_groups=mesh['xl'=2,'y'=4,'core'=2,'z'=4,'xh'=2] {'z','xh'}, dimensions={0} | all-to-all | bytes 32768 | tf_op jit(solution)/shard_map/all_to_all | solution.py:381
  187.2 1.3 fusion.2
  (45 shorter events, 0.5 us)
Async XLA Ops:
  0.6 75.7 %collective-permute-start.12 = (bf16[512,1024]{1,0:T(8,128)(2,1)}, bf16[512,1024]{1,0:T(8,128)(2,1)}, u32[]{:S(2)}, u32[]{:S(2)}) collective-permute-start(bf16[512,1024]{1,0:T(8,128)(2,1)} %refs_0_.1), channel_id=1, source_target_pairs={{0,64},{64,0},{1,65},{65,1},{2,66},{66,2},{3,67},{67,3},{4,68},{68... | collective-permute-start | bytes 3145736 | tf_op jit(solution)/shard_map/ppermute | solution.py:341
  2.3 91.3 %collective-permute-start.9 = (bf16[512,1024]{1,0:T(8,128)(2,1)}, bf16[512,1024]{1,0:T(8,128)(2,1)}, u32[]{:S(2)}, u32[]{:S(2)}) collective-permute-start(bf16[512,1024]{1,0:T(8,128)(2,1)} %refs_0_.1), channel_id=1, source_target_pairs={{0,16},{16,32},{32,48},{48,0},{1,17},{17,33},{33,49},{49,1},{2,18}... | collective-permute-start | bytes 3145736 | tf_op jit(solution)/shard_map/ppermute | solution.py:339
  3.9 0.7 copy-start
  4.6 7.0 %copy-start.1 = (s32[256]{0:T(256)S(1)}, s32[256]{0:T(256)}, u32[]{:S(2)}) copy-start(s32[256]{0:T(256)} %owner_ref.3) | copy-start | bytes 3076
  4.6 7.1 %copy-start.7 = (s32[256]{0:T(256)S(1)}, s32[256]{0:T(256)}, u32[]{:S(2)}) copy-start(s32[256]{0:T(256)} %param.18) | copy-start | bytes 3076
  4.6 8.2 %copy-start.8 = (s32[16]{0:T(128)S(1)}, s32[16]{0:T(128)}, u32[]{:S(2)}) copy-start(s32[16]{0:T(128)} %param.16) | copy-start | bytes 196
  7.3 32.6 %all-to-all-start = ((bf16[16,2,16,1024]{3,2,1,0:T(8,128)(2,1)}), bf16[16,2,16,1024]{3,2,1,0:T(8,128)(2,1)S(1)}, u32[]{:S(2)}, u32[]{:S(2)}) async-start(bf16[16,2,16,1024]{3,2,1,0:T(8,128)(2,1)} %dispatch.1), calls=%async_computation | async-start | bytes 2097152 | tf_op jit(solution)/shard_map/all_to_all | solution.py:337
  69.9 20.7 %all-to-all-start.1 = ((bf16[16,4,16,512]{3,2,1,0:T(8,128)(2,1)}), bf16[16,4,16,512]{3,2,1,0:T(8,128)(2,1)S(1)}, u32[]{:S(2)}, u32[]{:S(2)}) async-start(bf16[16,4,16,512]{3,2,1,0:T(8,128)(2,1)} %bitcast.3), calls=%async_computation.1 | async-start | bytes 2097152 | tf_op jit(solution)/shard_map/all_to_all | solution.py:358
  73.6 39.0 %collective-permute-start.13 = (bf16[512,1024]{1,0:T(8,128)(2,1)}, bf16[512,1024]{1,0:T(8,128)(2,1)S(1)}, u32[]{:S(2)}, u32[]{:S(2)}) collective-permute-start(bf16[512,1024]{1,0:T(8,128)(2,1)} %refs_0_.1), channel_id=1, source_target_pairs={{0,80},{16,96},{32,112},{48,64},{64,16},{80,32},{96,48},{112,0},{1... | collective-permute-start | bytes 3145736 | tf_op jit(solution)/shard_map/ppermute | solution.py:342
  76.3 40.3 %collective-permute-start.14 = (bf16[512,1024]{1,0:T(8,128)(2,1)}, bf16[512,1024]{1,0:T(8,128)(2,1)S(1)}, u32[]{:S(2)}, u32[]{:S(2)}) collective-permute-start(bf16[512,1024]{1,0:T(8,128)(2,1)} %collective-permute-done.12.refs_4_), channel_id=1, source_target_pairs={{0,48},{16,0},{32,16},{48,32},{1,49},{17,1},{33,17},{49,33},{2,50}... | collective-permute-start | bytes 3145736 | tf_op jit(solution)/shard_map/ppermute | solution.py:350
  78.1 55.4 %collective-permute-start.10 = (bf16[512,1024]{1,0:T(8,128)(2,1)}, bf16[512,1024]{1,0:T(8,128)(2,1)}, u32[]{:S(2)}, u32[]{:S(2)}) collective-permute-start(bf16[512,1024]{1,0:T(8,128)(2,1)} %refs_0_.1), channel_id=1, source_target_pairs={{0,48},{16,0},{32,16},{48,32},{1,49},{17,1},{33,17},{49,33},{2,50}... | collective-permute-start | bytes 3145736 | tf_op jit(solution)/shard_map/ppermute | solution.py:340
  91.6 25.1 %collective-permute-start.3 = (bf16[512,512]{1,0:T(8,128)(2,1)S(1)}, bf16[512,512]{1,0:T(8,128)(2,1)S(1)}, u32[]{:S(2)}, u32[]{:S(2)}) collective-permute-start(bf16[512,512]{1,0:T(8,128)(2,1)S(1)} %collect.1.own), channel_id=1, source_target_pairs={{0,2},{2,4},{4,6},{6,0},{1,3},{3,5},{5,7},{7,1},{8,10},{10,12},{12... | collective-permute-start | bytes 1572872 | tf_op jit(solution)/shard_map/ppermute | solution.py:361
  93.6 56.7 %collective-permute-start.11 = (bf16[512,1024]{1,0:T(8,128)(2,1)}, bf16[512,1024]{1,0:T(8,128)(2,1)S(1)}, u32[]{:S(2)}, u32[]{:S(2)}) collective-permute-start(bf16[512,1024]{1,0:T(8,128)(2,1)} %collective-permute-done.9.refs_1_), channel_id=1, source_target_pairs={{0,16},{16,32},{32,48},{48,0},{1,17},{17,33},{33,49},{49,1},{2,18}... | collective-permute-start | bytes 3145736 | tf_op jit(solution)/shard_map/ppermute | solution.py:349
  112.5 14.9 %collective-permute-start.5 = (bf16[512,512]{1,0:T(8,128)(2,1)S(1)}, bf16[512,512]{1,0:T(8,128)(2,1)S(1)}, u32[]{:S(2)}, u32[]{:S(2)}) collective-permute-start(bf16[512,512]{1,0:T(8,128)(2,1)S(1)} %collect.1.own), channel_id=1, source_target_pairs={{0,6},{2,0},{4,2},{6,4},{1,7},{3,1},{5,3},{7,5},{8,14},{10,8},{12,... | collective-permute-start | bytes 1572872 | tf_op jit(solution)/shard_map/ppermute | solution.py:362
  116.6 29.6 %collective-permute-start.15 = (bf16[256,1024]{1,0:T(8,128)(2,1)S(1)}, bf16[256,1024]{1,0:T(8,128)(2,1)S(1)}, u32[]{:S(2)}, u32[]{:S(2)}) collective-permute-start(bf16[256,1024]{1,0:T(8,128)(2,1)S(1)} %slice.18), channel_id=1, source_target_pairs={{0,16},{16,32},{32,48},{48,0},{1,17},{17,33},{33,49},{49,1},{2,18}... | collective-permute-start | bytes 1572872 | tf_op jit(solution)/shard_map/ppermute | solution.py:354
  116.7 33.6 %collective-permute-start = (bf16[512,512]{1,0:T(8,128)(2,1)S(1)}, bf16[512,512]{1,0:T(8,128)(2,1)S(1)}, u32[]{:S(2)}, u32[]{:S(2)}) collective-permute-start(bf16[512,512]{1,0:T(8,128)(2,1)S(1)} %collect.1.own), channel_id=1, source_target_pairs={{0,1},{1,0},{2,3},{3,2},{4,5},{5,4},{6,7},{7,6},{8,9},{9,8},{10,11... | collective-permute-start | bytes 1572872 | tf_op jit(solution)/shard_map/ppermute | solution.py:363
  127.5 32.5 %collective-permute-start.16 = (bf16[256,1024]{1,0:T(8,128)(2,1)S(1)}, bf16[256,1024]{1,0:T(8,128)(2,1)S(1)}, u32[]{:S(2)}, u32[]{:S(2)}) collective-permute-start(bf16[256,1024]{1,0:T(8,128)(2,1)S(1)} %slice.19), channel_id=1, source_target_pairs={{0,48},{16,0},{32,16},{48,32},{1,49},{17,1},{33,17},{49,33},{2,50}... | collective-permute-start | bytes 1572872 | tf_op jit(solution)/shard_map/ppermute | solution.py:355
  133.5 20.1 %collective-permute-start.4 = (bf16[256,512]{1,0:T(8,128)(2,1)S(1)}, bf16[256,512]{1,0:T(8,128)(2,1)S(1)}, u32[]{:S(2)}, u32[]{:S(2)}) collective-permute-start(bf16[256,512]{1,0:T(8,128)(2,1)S(1)} %slice.16), channel_id=1, source_target_pairs={{0,2},{2,4},{4,6},{6,0},{1,3},{3,5},{5,7},{7,1},{8,10},{10,12},{12... | collective-permute-start | bytes 786440 | tf_op jit(solution)/shard_map/ppermute | solution.py:365
  146.2 10.7 %collective-permute-start.6 = (bf16[256,512]{1,0:T(8,128)(2,1)S(1)}, bf16[256,512]{1,0:T(8,128)(2,1)S(1)}, u32[]{:S(2)}, u32[]{:S(2)}) collective-permute-start(bf16[256,512]{1,0:T(8,128)(2,1)S(1)} %slice.17), channel_id=1, source_target_pairs={{0,6},{2,0},{4,2},{6,4},{1,7},{3,1},{5,3},{7,5},{8,14},{10,8},{12,... | collective-permute-start | bytes 786440 | tf_op jit(solution)/shard_map/ppermute | solution.py:366
  150.3 17.9 %collective-permute-start.1 = (bf16[512,512]{1,0:T(8,128)(2,1)S(1)}, bf16[512,512]{1,0:T(8,128)(2,1)S(1)}, u32[]{:S(2)}, u32[]{:S(2)}) collective-permute-start(bf16[512,512]{1,0:T(8,128)(2,1)S(1)} %collective-permute-done.across), channel_id=1, source_target_pairs={{0,2},{2,4},{4,6},{6,0},{1,3},{3,5},{5,7},{7,1},{8,10},{10,12},{12... | collective-permute-start | bytes 1572872 | tf_op jit(solution)/shard_map/ppermute | solution.py:367
  150.3 17.9 %collective-permute-start.2 = (bf16[512,512]{1,0:T(8,128)(2,1)S(1)}, bf16[512,512]{1,0:T(8,128)(2,1)S(1)}, u32[]{:S(2)}, u32[]{:S(2)}) collective-permute-start(bf16[512,512]{1,0:T(8,128)(2,1)S(1)} %collective-permute-done.across), channel_id=1, source_target_pairs={{0,6},{2,0},{4,2},{6,4},{1,7},{3,1},{5,3},{7,5},{8,14},{10,8},{12,... | collective-permute-start | bytes 1572872 | tf_op jit(solution)/shard_map/ppermute | solution.py:368
  153.5 11.5 %collective-permute-start.7 = (bf16[256,512]{1,0:T(8,128)(2,1)S(1)}, bf16[256,512]{1,0:T(8,128)(2,1)S(1)}, u32[]{:S(2)}, u32[]{:S(2)}) collective-permute-start(bf16[256,512]{1,0:T(8,128)(2,1)S(1)} %collective-permute-done.4.far_a), channel_id=1, source_target_pairs={{0,1},{1,0},{2,3},{3,2},{4,5},{5,4},{6,7},{7,6},{8,9},{9,8},{10,11... | collective-permute-start | bytes 786440 | tf_op jit(solution)/shard_map/ppermute | solution.py:369
  157.0 11.2 %collective-permute-start.8 = (bf16[256,512]{1,0:T(8,128)(2,1)S(1)}, bf16[256,512]{1,0:T(8,128)(2,1)S(1)}, u32[]{:S(2)}, u32[]{:S(2)}) collective-permute-start(bf16[256,512]{1,0:T(8,128)(2,1)S(1)} %collective-permute-done.6.far_b), channel_id=1, source_target_pairs={{0,1},{1,0},{2,3},{3,2},{4,5},{5,4},{6,7},{7,6},{8,9},{9,8},{10,11... | collective-permute-start | bytes 786440 | tf_op jit(solution)/shard_map/ppermute | solution.py:370
  165.0 7.5 %copy-start.2 = (bf16[256,1024]{1,0:T(8,128)(2,1)S(1)}, bf16[256,1024]{1,0:T(8,128)(2,1)}, u32[]{:S(2)}) copy-start(bf16[256,1024]{1,0:T(8,128)(2,1)} %param.20) | copy-start | bytes 1572868
  165.0 7.5 %copy-start.4 = (bf16[256,1024]{1,0:T(8,128)(2,1)S(1)}, bf16[256,1024]{1,0:T(8,128)(2,1)}, u32[]{:S(2)}) copy-start(bf16[256,1024]{1,0:T(8,128)(2,1)} %param.11) | copy-start | bytes 1572868
  165.0 7.5 %copy-start.6 = (f32[1024]{0:T(1024)S(1)}, f32[1024]{0:T(1024)}, u32[]{:S(2)}) copy-start(f32[1024]{0:T(1024)} %param.19) | copy-start | bytes 12292
  170.5 16.7 %copy-start.5 = (bf16[256,1024]{1,0:T(8,128)(2,1)S(1)}, bf16[256,1024]{1,0:T(8,128)(2,1)}, u32[]{:S(2)}) copy-start(bf16[256,1024]{1,0:T(8,128)(2,1)} %param.21) | copy-start | bytes 1572868
  170.5 2.0 %collective-permute-start.17 = (bf16[256,1024]{1,0:T(8,128)(2,1)S(1)}, bf16[256,1024]{1,0:T(8,128)(2,1)S(1)}, u32[]{:S(2)}, u32[]{:S(2)}) collective-permute-start(bf16[256,1024]{1,0:T(8,128)(2,1)S(1)} %get-tuple-element.5), channel_id=1, source_target_pairs={{0,8},{8,0},{1,9},{9,1},{2,10},{10,2},{3,11},{11,3},{4,12},{12,4},... | collective-permute-start | bytes 1572872 | tf_op jit(solution)/shard_map/ppermute | solution.py:374
  173.0 15.5 %copy-start.3 = (bf16[256,1024]{1,0:T(8,128)(2,1)}, bf16[256,1024]{1,0:T(8,128)(2,1)S(1)}, u32[]{:S(2)}) copy-start(bf16[256,1024]{1,0:T(8,128)(2,1)S(1)} %get-tuple-element.10) | copy-start | bytes 1572868
where the time goes:
time: 189 us; the launch traced here: 188 us
  waiting for transfers between devices  82.5 us (44%)
  starting transfers between devices  42.5 us (22%)
  Pallas kernels  41.1 us (22%)
  blocking collectives  14.1 us (7%)
  other arithmetic  4.62 us (2%)
  local copies, waits for them, and re-layouts  1.96 us (1%)
    pallas_call x1, Pallas kernels, attend(): pl.pallas_call(attend_kernel, out_shape=pltpu.VMEM((SEQ // 2, 2, 2 * CAP,...  30 us
    all_to_all x1, waiting for transfers between devices, local(): lax.all_to_all(outgoing, SEQ_AXES, split_axis=0, concat_axis=0, tiled=True)  24.3 us
    ppermute x1, waiting for transfers between devices, local(): x_lo = lax.ppermute(w, ('xl', 'y'), SLANT)  18.9 us
    all_to_all x1, blocking collectives, local(): lax.all_to_all(copies, HEAD_AXES, split_axis=0, concat_axis=0, tiled=True)  14.1 us
    all_to_all x1, waiting for transfers between devices, local(): lax.all_to_all(context, SEQ_AXES, split_axis=0, concat_axis=0, tiled=True)  11 us
    ppermute x1, waiting for transfers between devices, local(): x_far_a = lax.ppermute(x_lo_top, 'y', UP)  10.9 us
    ppermute x1, waiting for transfers between devices, local(): above = lax.ppermute(own, 'z', DOWN)  7.65 us
    ppermute x1, waiting for transfers between devices, local(): w_hi = lax.ppermute(w, 'y', DOWN)  5.02 us
  transfers between devices with their start and end apart: 20, of which 9 were waited for; matrix products, arithmetic and copies ran while one was open for 2% of the time, Pallas kernels for 21%

commit v1 on v0

--- a/solution.py
+++ b/solution.py
@@ -346,17 +346,15 @@
     meta = jnp.stack([n_active, tiles])
     slots = received.reshape(SLOTS, BLK, width)
     context = attend(order, first, meta, slots, image_kv)
-    w_far = lax.ppermute(w_lo, "y", UP)
+    far_a = lax.ppermute(w_lo[:half], "y", UP)
+    far_b = lax.ppermute(w_hi[half:], "y", DOWN)
+    x_far = lax.ppermute(x_lo, "y", UP)
     x_hi = lax.ppermute(w_x, "y", DOWN)
 
-
-    x_lo_top, x_hi_end = x_lo[:half], x_hi[half:]
-    x_far_a = lax.ppermute(x_lo_top, "y", UP)
-    x_far_b = lax.ppermute(x_hi_end, "y", DOWN)
 
     context = context.reshape(SEQ, 2 * CAP, BLK, width // 2)
     returned = lax.all_to_all(context, SEQ_AXES, split_axis=0, concat_axis=0, tiled=True)
-    weights = assemble((w, w_lo, w_hi, w_far, w_x, x_lo, x_hi, x_far_a, x_far_b))
+    weights = assemble((w, w_lo, w_hi, far_a, far_b, w_x, x_lo, x_hi, x_far))
     own = collect(owners, returned)
     below = lax.ppermute(own, "z", UP)
     above = lax.ppermute(own, "z", DOWN)

time: 189 us -> 186 us (0.984)
  waiting for transfers between devices: 82.5 us -> 80.3 us
    ppermute x1, waiting for transfers between devices: 18.9 us -> 0.3 us  [local(): x_lo = lax.ppermute(w, ('xl', 'y'), SLANT)]
    ppermute x3, waiting for transfers between devices: 10.9 us -> 23.1 us  [the longest x1 15.2 us: local(): far_b = lax.ppermute(w_hi[half:], 'y', DOWN)]
    ppermute x1, waiting for transfers between devices: 5.02 us -> 14.4 us  [local(): w_hi = lax.ppermute(w, 'y', DOWN)]
    ppermute x1, waiting for transfers between devices: 7.65 us -> 0.01 us  [local(): above = lax.ppermute(own, 'z', DOWN)]
    ppermute x3, starting transfers between devices: 1.03 us -> 4.66 us  [the longest x1 2.28 us: local(): far_b = lax.ppermute(w_hi[half:], 'y', DOWN)]
    all_to_all x1, waiting for transfers between devices: 11 us -> 13.8 us  [local(): lax.all_to_all(context, SEQ_AXES, split_axis=0, concat_axis=0, tiled=True)]
    ppermute x1, starting transfers between devices: 2.77 us -> 0.27 us  [local(): x_lo = lax.ppermute(w, ('xl', 'y'), SLANT)]
  transfers between devices with their start and end apart: 20 -> 20, of which waited for: 9 -> 9; matrix products, arithmetic and copies ran while one was open for 2% -> 2% of each run, Pallas kernels for 21% -> 20%
where the time goes in v1:
time: 186 us
  waiting for transfers between devices  80.3 us (43%)
  starting transfers between devices  42.3 us (23%)
  Pallas kernels  39.5 us (21%)
  blocking collectives  14.2 us (8%)
  other arithmetic  4.74 us (3%)
  local copies, waits for them, and re-layouts  2.93 us (2%)
    pallas_call x1, Pallas kernels, attend(): pl.pallas_call(attend_kernel, out_shape=pltpu.VMEM((SEQ // 2, 2, 2 * CAP,...  29 us
    all_to_all x1, waiting for transfers between devices, local(): lax.all_to_all(outgoing, SEQ_AXES, split_axis=0, concat_axis=0, tiled=True)  24 us
    ppermute x1, waiting for transfers between devices, local(): far_b = lax.ppermute(w_hi[half:], 'y', DOWN)  15.2 us
    ppermute x1, waiting for transfers between devices, local(): w_hi = lax.ppermute(w, 'y', DOWN)  14.4 us
    all_to_all x1, blocking collectives, local(): lax.all_to_all(copies, HEAD_AXES, split_axis=0, concat_axis=0, tiled=True)  14.2 us
    all_to_all x1, waiting for transfers between devices, local(): lax.all_to_all(context, SEQ_AXES, split_axis=0, concat_axis=0, tiled=True)  13.8 us
    ppermute x1, waiting for transfers between devices, local(): far_a = lax.ppermute(w_lo[:half], 'y', UP)  7.92 us
    all_to_all x1, starting transfers between devices, local(): lax.all_to_all(outgoing, SEQ_AXES, split_axis=0, concat_axis=0, tiled=True)  4.29 us
  transfers between devices with their start and end apart: 20, of which 9 were waited for; matrix products, arithmetic and copies ran while one was open for 2% of the time, Pallas kernels for 20%

profile of v1, /device:TPU:0, one launch (start us, length us, event | category | flops | bytes accessed | tf_op | source)
XLA Modules:
  0.0 185.5 jit_solution(7402945361874576195)
XLA Ops:
  0.6 1.8 collective-permute-start.9
  2.4 1.5 collective-permute-start.13
  3.9 0.7 copy-done.2
  4.6 2.7 %dispatch.1 = bf16[16,2,16,1024]{3,2,1,0:T(8,128)(2,1)} custom-call(s32[256]{0:T(256)S(1)} %copy-done.2, bf16[256,1024]{1,0:T(8,128)(2,1)} %q_ref.1), custom_call_target="tpu_custom_call" | custom-call | tf_op jit(solution)/shard_map/dispatch/pallas_call | solution.py:72
  7.3 4.3 %all-to-all-start = ((bf16[16,2,16,1024]{3,2,1,0:T(8,128)(2,1)}), bf16[16,2,16,1024]{3,2,1,0:T(8,128)(2,1)S(1)}, u32[]{:S(2)}, u32[]{:S(2)}) async-start(bf16[16,2,16,1024]{3,2,1,0:T(8,128)(2,1)} %dispatch.1), calls=%async_computation | async-start | bytes 2097152 | tf_op jit(solution)/shard_map/all_to_all | solution.py:337
  11.8 0.4 convert_reduce_fusion
  12.1 0.1 select_reduce_fusion.2
  12.4 0.1 fusion.4
  12.6 0.1 copy.15
  12.7 0.1 reshape.99
  12.8 0.6 dynamic_slice.4
  13.4 0.7 convert_reduce_fusion.2
  14.1 1.3 pad_add_fusion.meta
  15.4 0.2 convert_reduce_fusion.1
  15.6 0.1 select_reduce_fusion
  15.7 24.0 %all-to-all-done = bf16[16,2,16,1024]{3,2,1,0:T(8,128)(2,1)S(1)} async-done(((bf16[16,2,16,1024]{3,2,1,0:T(8,128)(2,1)}), bf16[16,2,16,1024]{3,2,1,0:T(8,128)(2,1)S(1)}, u32[]{:S(2)}, u32[]{:S(2)}) %all-to-all-start) | async-done | bytes 1048608 | tf_op jit(solution)/shard_map/all_to_all | solution.py:337
  39.7 29.0 %attend.1 = bf16[8,2,4,16,512]{4,3,2,1,0:T(8,128)(2,1)S(1)} custom-call(s32[32]{0:T(128)S(1)} %get-tuple-element.9.order, s32[32]{0:T(128)S(1)} %get-tuple-element.8.first, s32[2]{0:T(128)S(1)} %pad_add_fusion.meta, bf16[32,16,1024]{2,1,0:T(8,128)(2,1)S(1)} %bitcast.8, bf16[1,2,6528,128]{3,2,1,0:T(8,128)(2,1)} %kv_ref.1), custom_call_target="tpu_custom_call" | custom-call | flops 10000000000 | bytes 10000000 | tf_op jit(solution)/shard_map/attend/pallas_call | solution.py:200
  68.7 1.0 copy-done.1
  69.7 3.7 %all-to-all-start.1 = ((bf16[16,4,16,512]{3,2,1,0:T(8,128)(2,1)}), bf16[16,4,16,512]{3,2,1,0:T(8,128)(2,1)S(1)}, u32[]{:S(2)}, u32[]{:S(2)}) async-start(bf16[16,4,16,512]{3,2,1,0:T(8,128)(2,1)} %bitcast.9), calls=%async_computation.1 | async-start | bytes 2097152 | tf_op jit(solution)/shard_map/all_to_all | solution.py:356
  73.4 3.1 %collective-permute-start.10 = (bf16[512,1024]{1,0:T(8,128)(2,1)}, bf16[512,1024]{1,0:T(8,128)(2,1)S(1)}, u32[]{:S(2)}, u32[]{:S(2)}) collective-permute-start(bf16[512,1024]{1,0:T(8,128)(2,1)} %refs_0_.1), channel_id=1, source_target_pairs={{0,48},{16,0},{32,16},{48,32},{1,49},{17,1},{33,17},{49,33},{2,50}... | collective-permute-start | bytes 3145736 | tf_op jit(solution)/shard_map/ppermute | solution.py:340
  76.4 0.3 collective-permute-start.14
  76.7 13.8 %all-to-all-done.1.c_ref = bf16[16,4,16,512]{3,2,1,0:T(8,128)(2,1)S(1)} async-done(((bf16[16,4,16,512]{3,2,1,0:T(8,128)(2,1)}), bf16[16,4,16,512]{3,2,1,0:T(8,128)(2,1)S(1)}, u32[]{:S(2)}, u32[]{:S(2)}) %all-to-all-start.1) | async-done | bytes 1048608 | tf_op jit(solution)/shard_map/all_to_all | solution.py:356
  90.4 1.0 collect.1.own
  91.4 2.0 %collective-permute-start.3 = (bf16[512,512]{1,0:T(8,128)(2,1)S(1)}, bf16[512,512]{1,0:T(8,128)(2,1)S(1)}, u32[]{:S(2)}, u32[]{:S(2)}) collective-permute-start(bf16[512,512]{1,0:T(8,128)(2,1)S(1)} %collect.1.own), channel_id=1, source_target_pairs={{0,2},{2,4},{4,6},{6,0},{1,3},{3,5},{5,7},{7,1},{8,10},{10,12},{12... | collective-permute-start | bytes 1572872 | tf_op jit(solution)/shard_map/ppermute | solution.py:359
  93.4 2.2 %collective-permute-start.5 = (bf16[512,512]{1,0:T(8,128)(2,1)S(1)}, bf16[512,512]{1,0:T(8,128)(2,1)S(1)}, u32[]{:S(2)}, u32[]{:S(2)}) collective-permute-start(bf16[512,512]{1,0:T(8,128)(2,1)S(1)} %collect.1.own), channel_id=1, source_target_pairs={{0,6},{2,0},{4,2},{6,4},{1,7},{3,1},{5,3},{7,5},{8,14},{10,8},{12,... | collective-permute-start | bytes 1572872 | tf_op jit(solution)/shard_map/ppermute | solution.py:360
  95.6 0.6 collective-permute-start.15
  96.3 14.4 %collective-permute-done.10.refs_2_ = bf16[512,1024]{1,0:T(8,128)(2,1)S(1)} collective-permute-done((bf16[512,1024]{1,0:T(8,128)(2,1)}, bf16[512,1024]{1,0:T(8,128)(2,1)S(1)}, u32[]{:S(2)}, u32[]{:S(2)}) %collective-permute-start.10) | collective-permute-done | bytes 1048608 | tf_op jit(solution)/shard_map/ppermute | solution.py:340
  110.7 1.4 collective-permute-start.11
  112.1 0.3 collective-permute-done.14.refs_6_
  112.4 1.0 collective-permute-start.16
  113.4 2.3 %collective-permute-start.12 = (bf16[256,1024]{1,0:T(8,128)(2,1)S(1)}, bf16[256,1024]{1,0:T(8,128)(2,1)S(1)}, u32[]{:S(2)}, u32[]{:S(2)}) collective-permute-start(bf16[256,1024]{1,0:T(8,128)(2,1)S(1)} %slice.19), channel_id=1, source_target_pairs={{0,48},{16,0},{32,16},{48,32},{1,49},{17,1},{33,17},{49,33},{2,50}... | collective-permute-start | bytes 1572872 | tf_op jit(solution)/shard_map/ppermute | solution.py:350
  115.7 3.0 %collective-permute-start = (bf16[512,512]{1,0:T(8,128)(2,1)S(1)}, bf16[512,512]{1,0:T(8,128)(2,1)S(1)}, u32[]{:S(2)}, u32[]{:S(2)}) collective-permute-start(bf16[512,512]{1,0:T(8,128)(2,1)S(1)} %collect.1.own), channel_id=1, source_target_pairs={{0,1},{1,0},{2,3},{3,2},{4,5},{5,4},{6,7},{7,6},{8,9},{9,8},{10,11... | collective-permute-start | bytes 1572872 | tf_op jit(solution)/shard_map/ppermute | solution.py:361
  118.8 7.9 %collective-permute-done.11.refs_3_ = bf16[256,1024]{1,0:T(8,128)(2,1)S(1)} collective-permute-done((bf16[256,1024]{1,0:T(8,128)(2,1)S(1)}, bf16[256,1024]{1,0:T(8,128)(2,1)S(1)}, u32[]{:S(2)}, u32[]{:S(2)}) %collective-permute-start.11) | collective-permute-done | bytes 524320 | tf_op jit(solution)/shard_map/ppermute | solution.py:349
  126.7 1.9 %collective-permute-start.4 = (bf16[256,512]{1,0:T(8,128)(2,1)S(1)}, bf16[256,512]{1,0:T(8,128)(2,1)S(1)}, u32[]{:S(2)}, u32[]{:S(2)}) collective-permute-start(bf16[256,512]{1,0:T(8,128)(2,1)S(1)} %slice.16), channel_id=1, source_target_pairs={{0,2},{2,4},{4,6},{6,0},{1,3},{3,5},{5,7},{7,1},{8,10},{10,12},{12... | collective-permute-start | bytes 786440 | tf_op jit(solution)/shard_map/ppermute | solution.py:363
  128.6 15.2 %collective-permute-done.12.refs_4_ = bf16[256,1024]{1,0:T(8,128)(2,1)S(1)} collective-permute-done((bf16[256,1024]{1,0:T(8,128)(2,1)S(1)}, bf16[256,1024]{1,0:T(8,128)(2,1)S(1)}, u32[]{:S(2)}, u32[]{:S(2)}) %collective-permute-start.12) | collective-permute-done | bytes 524320 | tf_op jit(solution)/shard_map/ppermute | solution.py:350
  143.8 4.0 %collective-permute-start.6 = (bf16[256,512]{1,0:T(8,128)(2,1)S(1)}, bf16[256,512]{1,0:T(8,128)(2,1)S(1)}, u32[]{:S(2)}, u32[]{:S(2)}) collective-permute-start(bf16[256,512]{1,0:T(8,128)(2,1)S(1)} %slice.17), channel_id=1, source_target_pairs={{0,6},{2,0},{4,2},{6,4},{1,7},{3,1},{5,3},{7,5},{8,14},{10,8},{12,... | collective-permute-start | bytes 786440 | tf_op jit(solution)/shard_map/ppermute | solution.py:364
  147.9 3.2 %collective-permute-start.2 = (bf16[512,512]{1,0:T(8,128)(2,1)S(1)}, bf16[512,512]{1,0:T(8,128)(2,1)S(1)}, u32[]{:S(2)}, u32[]{:S(2)}) collective-permute-start(bf16[512,512]{1,0:T(8,128)(2,1)S(1)} %collective-permute-done.across), channel_id=1, source_target_pairs={{0,6},{2,0},{4,2},{6,4},{1,7},{3,1},{5,3},{7,5},{8,14},{10,8},{12,... | collective-permute-start | bytes 1572872 | tf_op jit(solution)/shard_map/ppermute | solution.py:366
  151.1 3.0 %collective-permute-start.7 = (bf16[256,512]{1,0:T(8,128)(2,1)S(1)}, bf16[256,512]{1,0:T(8,128)(2,1)S(1)}, u32[]{:S(2)}, u32[]{:S(2)}) collective-permute-start(bf16[256,512]{1,0:T(8,128)(2,1)S(1)} %collective-permute-done.4.far_a), channel_id=1, source_target_pairs={{0,1},{1,0},{2,3},{3,2},{4,5},{5,4},{6,7},{7,6},{8,9},{9,8},{10,11... | collective-permute-start | bytes 786440 | tf_op jit(solution)/shard_map/ppermute | solution.py:367
  154.1 0.4 collective-permute-done.6.far_b
  154.6 3.0 %collective-permute-start.8 = (bf16[256,512]{1,0:T(8,128)(2,1)S(1)}, bf16[256,512]{1,0:T(8,128)(2,1)S(1)}, u32[]{:S(2)}, u32[]{:S(2)}) collective-permute-start(bf16[256,512]{1,0:T(8,128)(2,1)S(1)} %collective-permute-done.6.far_b), channel_id=1, source_target_pairs={{0,1},{1,0},{2,3},{3,2},{4,5},{5,4},{6,7},{7,6},{8,9},{9,8},{10,11... | collective-permute-start | bytes 786440 | tf_op jit(solution)/shard_map/ppermute | solution.py:368
  157.6 2.1 %assemble.1.w = bf16[8,512,1024]{2,1,0:T(8,128)(2,1)S(1)} custom-call(bf16[512,1024]{1,0:T(8,128)(2,1)S(1)} %copy-done, bf16[512,1024]{1,0:T(8,128)(2,1)S(1)} %collective-permute-done.9.refs_1_, bf16[512,1024]{1,0:T(8,128)(2,1)S(1)} %collective-permute-done.10.refs_2_, bf16[256,1024]{1,0:T(8,128)(2,1)S(1)} %collective-permute-done.11.refs_3_, ...), custom_call_target="tpu_custom_call" | custom-call | tf_op jit(solution)/shard_map/assemble/pallas_call | solution.py:242
  159.7 2.3 %project_first.1.total = f32[512,1024]{1,0:T(8,128)S(1)} custom-call(bf16[512,512]{1,0:T(8,128)(2,1)S(1)} %collect.1.own, bf16[512,512]{1,0:T(8,128)(2,1)S(1)} %collective-permute-done.3.below, bf16[512,512]{1,0:T(8,128)(2,1)S(1)} %collective-permute-done.5.above, bf16[512,512]{1,0:T(8,128)(2,1)S(1)} %collective-permute-done.across, ...), custom_call_target="tpu_custom_call" | custom-call | tf_op jit(solution)/shard_map/project_first/pallas_call | solution.py:266
  162.1 3.1 %collective-permute-done.8.over_b = bf16[256,512]{1,0:T(8,128)(2,1)S(1)} collective-permute-done((bf16[256,512]{1,0:T(8,128)(2,1)S(1)}, bf16[256,512]{1,0:T(8,128)(2,1)S(1)}, u32[]{:S(2)}, u32[]{:S(2)}) %collective-permute-start.8) | collective-permute-done | bytes 262176 | tf_op jit(solution)/shard_map/ppermute | solution.py:368
  165.2 2.3 %project_last.1 = (f32[256,1024]{1,0:T(8,128)S(1)}, bf16[256,1024]{1,0:T(8,128)(2,1)S(1)}) custom-call(bf16[512,512]{1,0:T(8,128)(2,1)S(1)} %collective-permute-done.1.below, bf16[512,512]{1,0:T(8,128)(2,1)S(1)} %collective-permute-done.2.above, bf16[256,512]{1,0:T(8,128)(2,1)S(1)} %collective-permute-done.4.far_a, ...), custom_call_target="tpu_custom_call" | custom-call | tf_op jit(solution)/shard_map/project_last/pallas_call | solution.py:289
  168.3 1.2 collective-permute-done.17
  169.5 0.5 fusion
  170.0 14.2 %all_to_all.15 = f32[8,2,256]{2,1,0:T(2,128)S(1)} all-to-all(f32[8,2,256]{2,1,0:T(2,128)S(1)} %broadcast_in_dim.64), channel_id=1, replica_groups=mesh['xl'=2,'y'=4,'core'=2,'z'=4,'xh'=2] {'z','xh'}, dimensions={0} | all-to-all | bytes 32768 | tf_op jit(solution)/shard_map/all_to_all | solution.py:379
  184.2 1.3 fusion.2
  (49 shorter events, 0.7 us)
Async XLA Ops:
  0.6 92.8 %collective-permute-start.9 = (bf16[512,1024]{1,0:T(8,128)(2,1)}, bf16[512,1024]{1,0:T(8,128)(2,1)S(1)}, u32[]{:S(2)}, u32[]{:S(2)}) collective-permute-start(bf16[512,1024]{1,0:T(8,128)(2,1)} %refs_0_.1), channel_id=1, source_target_pairs={{0,16},{16,32},{32,48},{48,0},{1,17},{17,33},{33,49},{49,1},{2,18}... | collective-permute-start | bytes 3145736 | tf_op jit(solution)/shard_map/ppermute | solution.py:339
  2.4 93.2 %collective-permute-start.13 = (bf16[512,1024]{1,0:T(8,128)(2,1)}, bf16[512,1024]{1,0:T(8,128)(2,1)}, u32[]{:S(2)}, u32[]{:S(2)}) collective-permute-start(bf16[512,1024]{1,0:T(8,128)(2,1)} %refs_0_.1), channel_id=1, source_target_pairs={{0,64},{64,0},{1,65},{65,1},{2,66},{66,2},{3,67},{67,3},{4,68},{68... | collective-permute-start | bytes 3145736 | tf_op jit(solution)/shard_map/ppermute | solution.py:341
  3.9 0.7 copy-start.2
  4.6 7.0 %copy-start.3 = (s32[256]{0:T(256)S(1)}, s32[256]{0:T(256)}, u32[]{:S(2)}) copy-start(s32[256]{0:T(256)} %owner_ref.3) | copy-start | bytes 3076
  4.6 7.1 %copy-start.9 = (s32[256]{0:T(256)S(1)}, s32[256]{0:T(256)}, u32[]{:S(2)}) copy-start(s32[256]{0:T(256)} %param.18) | copy-start | bytes 3076
  4.6 8.2 %copy-start.10 = (s32[16]{0:T(128)S(1)}, s32[16]{0:T(128)}, u32[]{:S(2)}) copy-start(s32[16]{0:T(128)} %param.16) | copy-start | bytes 196
  7.3 32.4 %all-to-all-start = ((bf16[16,2,16,1024]{3,2,1,0:T(8,128)(2,1)}), bf16[16,2,16,1024]{3,2,1,0:T(8,128)(2,1)S(1)}, u32[]{:S(2)}, u32[]{:S(2)}) async-start(bf16[16,2,16,1024]{3,2,1,0:T(8,128)(2,1)} %dispatch.1), calls=%async_computation | async-start | bytes 2097152 | tf_op jit(solution)/shard_map/all_to_all | solution.py:337
  68.7 1.0 copy-start.1
  69.7 20.7 %all-to-all-start.1 = ((bf16[16,4,16,512]{3,2,1,0:T(8,128)(2,1)}), bf16[16,4,16,512]{3,2,1,0:T(8,128)(2,1)S(1)}, u32[]{:S(2)}, u32[]{:S(2)}) async-start(bf16[16,4,16,512]{3,2,1,0:T(8,128)(2,1)} %bitcast.9), calls=%async_computation.1 | async-start | bytes 2097152 | tf_op jit(solution)/shard_map/all_to_all | solution.py:356
  73.4 37.3 %collective-permute-start.10 = (bf16[512,1024]{1,0:T(8,128)(2,1)}, bf16[512,1024]{1,0:T(8,128)(2,1)S(1)}, u32[]{:S(2)}, u32[]{:S(2)}) collective-permute-start(bf16[512,1024]{1,0:T(8,128)(2,1)} %refs_0_.1), channel_id=1, source_target_pairs={{0,48},{16,0},{32,16},{48,32},{1,49},{17,1},{33,17},{49,33},{2,50}... | collective-permute-start | bytes 3145736 | tf_op jit(solution)/shard_map/ppermute | solution.py:340
  76.4 36.0 %collective-permute-start.14 = (bf16[512,1024]{1,0:T(8,128)(2,1)}, bf16[512,1024]{1,0:T(8,128)(2,1)}, u32[]{:S(2)}, u32[]{:S(2)}) collective-permute-start(bf16[512,1024]{1,0:T(8,128)(2,1)} %refs_0_.1), channel_id=1, source_target_pairs={{0,80},{16,96},{32,112},{48,64},{64,16},{80,32},{96,48},{112,0},{1... | collective-permute-start | bytes 3145736 | tf_op jit(solution)/shard_map/ppermute | solution.py:342
  90.4 67.2 %copy-start = (bf16[512,1024]{1,0:T(8,128)(2,1)S(1)}, bf16[512,1024]{1,0:T(8,128)(2,1)}, u32[]{:S(2)}) copy-start(bf16[512,1024]{1,0:T(8,128)(2,1)} %refs_0_.1) | copy-start | bytes 3145732
  91.4 22.0 %collective-permute-start.3 = (bf16[512,512]{1,0:T(8,128)(2,1)S(1)}, bf16[512,512]{1,0:T(8,128)(2,1)S(1)}, u32[]{:S(2)}, u32[]{:S(2)}) collective-permute-start(bf16[512,512]{1,0:T(8,128)(2,1)S(1)} %collect.1.own), channel_id=1, source_target_pairs={{0,2},{2,4},{4,6},{6,0},{1,3},{3,5},{5,7},{7,1},{8,10},{10,12},{12... | collective-permute-start | bytes 1572872 | tf_op jit(solution)/shard_map/ppermute | solution.py:359
  93.4 22.3 %collective-permute-start.5 = (bf16[512,512]{1,0:T(8,128)(2,1)S(1)}, bf16[512,512]{1,0:T(8,128)(2,1)S(1)}, u32[]{:S(2)}, u32[]{:S(2)}) collective-permute-start(bf16[512,512]{1,0:T(8,128)(2,1)S(1)} %collect.1.own), channel_id=1, source_target_pairs={{0,6},{2,0},{4,2},{6,4},{1,7},{3,1},{5,3},{7,5},{8,14},{10,8},{12,... | collective-permute-start | bytes 1572872 | tf_op jit(solution)/shard_map/ppermute | solution.py:360
  95.6 52.2 %collective-permute-start.15 = (bf16[512,1024]{1,0:T(8,128)(2,1)}, bf16[512,1024]{1,0:T(8,128)(2,1)S(1)}, u32[]{:S(2)}, u32[]{:S(2)}) collective-permute-start(bf16[512,1024]{1,0:T(8,128)(2,1)} %collective-permute-done.13.refs_5_), channel_id=1, source_target_pairs={{0,48},{16,0},{32,16},{48,32},{1,49},{17,1},{33,17},{49,33},{2,50}... | collective-permute-start | bytes 3145736 | tf_op jit(solution)/shard_map/ppermute | solution.py:352
  110.7 16.0 %collective-permute-start.11 = (bf16[256,1024]{1,0:T(8,128)(2,1)S(1)}, bf16[256,1024]{1,0:T(8,128)(2,1)S(1)}, u32[]{:S(2)}, u32[]{:S(2)}) collective-permute-start(bf16[256,1024]{1,0:T(8,128)(2,1)S(1)} %slice.18), channel_id=1, source_target_pairs={{0,16},{16,32},{32,48},{48,0},{1,17},{17,33},{33,49},{49,1},{2,18}... | collective-permute-start | bytes 1572872 | tf_op jit(solution)/shard_map/ppermute | solution.py:349
  112.4 45.1 %collective-permute-start.16 = (bf16[512,1024]{1,0:T(8,128)(2,1)}, bf16[512,1024]{1,0:T(8,128)(2,1)S(1)}, u32[]{:S(2)}, u32[]{:S(2)}) collective-permute-start(bf16[512,1024]{1,0:T(8,128)(2,1)} %collective-permute-done.14.refs_6_), channel_id=1, source_target_pairs={{0,16},{16,32},{32,48},{48,0},{1,17},{17,33},{33,49},{49,1},{2,18}... | collective-permute-start | bytes 3145736 | tf_op jit(solution)/shard_map/ppermute | solution.py:351
  113.4 30.4 %collective-permute-start.12 = (bf16[256,1024]{1,0:T(8,128)(2,1)S(1)}, bf16[256,1024]{1,0:T(8,128)(2,1)S(1)}, u32[]{:S(2)}, u32[]{:S(2)}) collective-permute-start(bf16[256,1024]{1,0:T(8,128)(2,1)S(1)} %slice.19), channel_id=1, source_target_pairs={{0,48},{16,0},{32,16},{48,32},{1,49},{17,1},{33,17},{49,33},{2,50}... | collective-permute-start | bytes 1572872 | tf_op jit(solution)/shard_map/ppermute | solution.py:350
  115.7 32.2 %collective-permute-start = (bf16[512,512]{1,0:T(8,128)(2,1)S(1)}, bf16[512,512]{1,0:T(8,128)(2,1)S(1)}, u32[]{:S(2)}, u32[]{:S(2)}) collective-permute-start(bf16[512,512]{1,0:T(8,128)(2,1)S(1)} %collect.1.own), channel_id=1, source_target_pairs={{0,1},{1,0},{2,3},{3,2},{4,5},{5,4},{6,7},{7,6},{8,9},{9,8},{10,11... | collective-permute-start | bytes 1572872 | tf_op jit(solution)/shard_map/ppermute | solution.py:361
  126.7 24.4 %collective-permute-start.4 = (bf16[256,512]{1,0:T(8,128)(2,1)S(1)}, bf16[256,512]{1,0:T(8,128)(2,1)S(1)}, u32[]{:S(2)}, u32[]{:S(2)}) collective-permute-start(bf16[256,512]{1,0:T(8,128)(2,1)S(1)} %slice.16), channel_id=1, source_target_pairs={{0,2},{2,4},{4,6},{6,0},{1,3},{3,5},{5,7},{7,1},{8,10},{10,12},{12... | collective-permute-start | bytes 786440 | tf_op jit(solution)/shard_map/ppermute | solution.py:363
  143.8 10.7 %collective-permute-start.6 = (bf16[256,512]{1,0:T(8,128)(2,1)S(1)}, bf16[256,512]{1,0:T(8,128)(2,1)S(1)}, u32[]{:S(2)}, u32[]{:S(2)}) collective-permute-start(bf16[256,512]{1,0:T(8,128)(2,1)S(1)} %slice.17), channel_id=1, source_target_pairs={{0,6},{2,0},{4,2},{6,4},{1,7},{3,1},{5,3},{7,5},{8,14},{10,8},{12,... | collective-permute-start | bytes 786440 | tf_op jit(solution)/shard_map/ppermute | solution.py:364
  147.9 17.3 %collective-permute-start.1 = (bf16[512,512]{1,0:T(8,128)(2,1)S(1)}, bf16[512,512]{1,0:T(8,128)(2,1)S(1)}, u32[]{:S(2)}, u32[]{:S(2)}) collective-permute-start(bf16[512,512]{1,0:T(8,128)(2,1)S(1)} %collective-permute-done.across), channel_id=1, source_target_pairs={{0,2},{2,4},{4,6},{6,0},{1,3},{3,5},{5,7},{7,1},{8,10},{10,12},{12... | collective-permute-start | bytes 1572872 | tf_op jit(solution)/shard_map/ppermute | solution.py:365
  147.9 17.3 %collective-permute-start.2 = (bf16[512,512]{1,0:T(8,128)(2,1)S(1)}, bf16[512,512]{1,0:T(8,128)(2,1)S(1)}, u32[]{:S(2)}, u32[]{:S(2)}) collective-permute-start(bf16[512,512]{1,0:T(8,128)(2,1)S(1)} %collective-permute-done.across), channel_id=1, source_target_pairs={{0,6},{2,0},{4,2},{6,4},{1,7},{3,1},{5,3},{7,5},{8,14},{10,8},{12,... | collective-permute-start | bytes 1572872 | tf_op jit(solution)/shard_map/ppermute | solution.py:366
  151.1 11.0 %collective-permute-start.7 = (bf16[256,512]{1,0:T(8,128)(2,1)S(1)}, bf16[256,512]{1,0:T(8,128)(2,1)S(1)}, u32[]{:S(2)}, u32[]{:S(2)}) collective-permute-start(bf16[256,512]{1,0:T(8,128)(2,1)S(1)} %collective-permute-done.4.far_a), channel_id=1, source_target_pairs={{0,1},{1,0},{2,3},{3,2},{4,5},{5,4},{6,7},{7,6},{8,9},{9,8},{10,11... | collective-permute-start | bytes 786440 | tf_op jit(solution)/shard_map/ppermute | solution.py:367
  154.6 10.6 %collective-permute-start.8 = (bf16[256,512]{1,0:T(8,128)(2,1)S(1)}, bf16[256,512]{1,0:T(8,128)(2,1)S(1)}, u32[]{:S(2)}, u32[]{:S(2)}) collective-permute-start(bf16[256,512]{1,0:T(8,128)(2,1)S(1)} %collective-permute-done.6.far_b), channel_id=1, source_target_pairs={{0,1},{1,0},{2,3},{3,2},{4,5},{5,4},{6,7},{7,6},{8,9},{9,8},{10,11... | collective-permute-start | bytes 786440 | tf_op jit(solution)/shard_map/ppermute | solution.py:368
  162.0 7.5 %copy-start.4 = (bf16[256,1024]{1,0:T(8,128)(2,1)S(1)}, bf16[256,1024]{1,0:T(8,128)(2,1)}, u32[]{:S(2)}) copy-start(bf16[256,1024]{1,0:T(8,128)(2,1)} %param.20) | copy-start | bytes 1572868
  162.0 7.5 %copy-start.6 = (bf16[256,1024]{1,0:T(8,128)(2,1)S(1)}, bf16[256,1024]{1,0:T(8,128)(2,1)}, u32[]{:S(2)}) copy-start(bf16[256,1024]{1,0:T(8,128)(2,1)} %param.11) | copy-start | bytes 1572868
  162.1 7.4 %copy-start.8 = (f32[1024]{0:T(1024)S(1)}, f32[1024]{0:T(1024)}, u32[]{:S(2)}) copy-start(f32[1024]{0:T(1024)} %param.19) | copy-start | bytes 12292
  167.5 16.7 %copy-start.7 = (bf16[256,1024]{1,0:T(8,128)(2,1)S(1)}, bf16[256,1024]{1,0:T(8,128)(2,1)}, u32[]{:S(2)}) copy-start(bf16[256,1024]{1,0:T(8,128)(2,1)} %param.21) | copy-start | bytes 1572868
  167.5 2.0 %collective-permute-start.17 = (bf16[256,1024]{1,0:T(8,128)(2,1)S(1)}, bf16[256,1024]{1,0:T(8,128)(2,1)S(1)}, u32[]{:S(2)}, u32[]{:S(2)}) collective-permute-start(bf16[256,1024]{1,0:T(8,128)(2,1)S(1)} %get-tuple-element.5), channel_id=1, source_target_pairs={{0,8},{8,0},{1,9},{9,1},{2,10},{10,2},{3,11},{11,3},{4,12},{12,4},... | collective-permute-start | bytes 1572872 | tf_op jit(solution)/shard_map/ppermute | solution.py:372
  170.0 15.5 %copy-start.5 = (bf16[256,1024]{1,0:T(8,128)(2,1)}, bf16[256,1024]{1,0:T(8,128)(2,1)S(1)}, u32[]{:S(2)}) copy-start(bf16[256,1024]{1,0:T(8,128)(2,1)S(1)} %get-tuple-element.10) | copy-start | bytes 1572868
